TPU v7x, 128 devices: a whole 4x4x4 slice. The times are simulated.
128 devices in a mesh: attn: 8 (over x, core), ffn: 16 (over y, z).
Axes of the slice: x: 4, y: 4, z: 4, core: 2. Of those that a mesh axis runs over, the one named last changes fastest.
Arguments:
- queries: bfloat16 [1024, 2, 64, 576], P(('attn', 'ffn')), may hold values from -9 to 9
- latent_cache: bfloat16 [1024, 512, 576], P(('attn', 'ffn')), may hold values from -4 to 4
- fresh_latent: bfloat16 [1024, 2, 576], P(('attn', 'ffn')), may hold values from -4 to 4
- lengths: int32 [1024], P(('attn', 'ffn')), may hold values from 1 to 512, 262144 in all
- handoff: int32 [16, 8], P('ffn'), may hold values 0 or 1
- residual: bfloat16 [1024, 2, 7168], P(('attn', 'ffn')), may hold values from -30 to 30
- value_up_matrix: bfloat16 [64, 512, 128], P('ffn'), may hold values from -0.5 to 0.5
- output_weight: bfloat16 [8192, 7168], P('ffn'), may hold values from -0.1875 to 0.1875
- norm_gain: float32 [7168], replicated, may hold values from 0.3 to 3
- router: bfloat16 [7168, 16], replicated, may hold values from -0.0625 to 0.0625
- expert_ids: int32 [1024, 2, 2], P('attn'), may hold values from 0 to 15, all different within a row; in each aligned block of 256 rows (0 to 255, 256 to 511, ..., all dimensions but the last counted through in order) at most 64 rows name the same one
- gate_weight: bfloat16 [16, 7168, 2048], P('ffn', None, 'attn'), may hold values from -0.0625 to 0.0625
- up_weight: bfloat16 [16, 7168, 2048], P('ffn', None, 'attn'), may hold values from -0.0625 to 0.0625
- down_weight: bfloat16 [16, 2048, 7168], P('ffn', 'attn'), may hold values from -0.125 to 0.125
Outputs:
- attended: bfloat16 [1024, 2, 7168], P(('attn', 'ffn'))
- expert_out: bfloat16 [1024, 2, 7168], P(('attn', 'ffn'))
Inputs may be any that keep to these rules, and one draw needn't show every extreme that they name: `expert_ids`: the 2 ids of a token differ. In each aligned block of 256 tokens (the requests of one index of attn, all new tokens of each, in order) no expert is chosen by more than 64 tokens, and some expert is chosen by exactly 64 in some block.
All inputs are finite; a program needn't handle non-finite values. No bound on the sum of `lengths` or of `handoff` on one device may be relied on, other than what follows from the above.
Results may differ from a plain program's by a relative error of at most 0.014.
Values may be sent and summed in bfloat16 or wider, within the bound.
A program may use at most 128 MiB of HBM per device.

v0:
```python
import jax
import jax.numpy as jnp
from jax import lax
from jax.sharding import PartitionSpec as P

KV_RANK = 512


score_scale = 192.0 ** (-0.5)
norm_epsilon = 1e-06


def shifted(value, axis, by):
    count = lax.axis_size(axis)
    return lax.ppermute(value, axis, [(i, (i + by) % count) for i in range(count)])


def attend_block(queries, latent_cache, fresh_latent, lengths):
    req_count, steps_here, heads_here, latent_width = queries.shape
    cache_span = latent_cache.shape[1]
    row_count = steps_here * heads_here
    rows_flat = queries.reshape(req_count, row_count, latent_width)
    old_scores = (
        jnp.einsum("rqc,rnc->rqn", rows_flat, latent_cache, preferred_element_type=jnp.float32)
        * score_scale
    )
    position = lax.broadcasted_iota(jnp.int32, (1, 1, cache_span), 2)
    old_scores = jnp.where(position < lengths[:, None, None], old_scores, -jnp.inf)
    new_scores = (
        jnp.einsum("rqc,rjc->rqj", rows_flat, fresh_latent, preferred_element_type=jnp.float32)
        * score_scale
    )
    row_step = lax.broadcasted_iota(jnp.int32, (1, row_count, steps_here), 1) // heads_here
    column_step = lax.broadcasted_iota(jnp.int32, (1, row_count, steps_here), 2)
    new_scores = jnp.where(column_step <= row_step, new_scores, -jnp.inf)
    row_peak = jnp.maximum(jnp.max(old_scores, axis=2), jnp.max(new_scores, axis=2))[:, :, None]
    old_exp = jnp.exp(old_scores - row_peak)
    new_exp = jnp.exp(new_scores - row_peak)
    denominator = jnp.sum(old_exp, axis=2, keepdims=True) + jnp.sum(new_exp, axis=2, keepdims=True)
    old_probs = (old_exp / denominator).astype(jnp.bfloat16)
    new_probs = (new_exp / denominator).astype(jnp.bfloat16)
    latent_mix = jnp.einsum(
        "rqn,rnc->rqc", old_probs, latent_cache[:, :, :KV_RANK], preferred_element_type=jnp.float32
    )
    latent_mix = latent_mix + jnp.einsum(
        "rqj,rjc->rqc", new_probs, fresh_latent[:, :, :KV_RANK], preferred_element_type=jnp.float32
    )
    return latent_mix.astype(jnp.bfloat16).reshape(req_count, steps_here, heads_here, KV_RANK)


def rms_normalize(state, norm_gain):
    scale_rows = lax.rsqrt(jnp.mean(state * state, axis=-1, keepdims=True) + norm_epsilon)
    return (state * scale_rows * norm_gain).astype(jnp.bfloat16)


def local(
    queries,
    latent_cache,
    fresh_latent,
    lengths,
    handoff,
    residual,
    value_up_matrix,
    output_weight,
    norm_gain,
    router,
    expert_ids,
    gate_weight,
    up_weight,
    down_weight,
):
    moved_flag = handoff[0] == 1
    moved_here = moved_flag[:, None, None, None]
    arrived = shifted((queries, latent_cache, fresh_latent, lengths), "attn", 1)
    queries_now = jnp.where(moved_here, arrived[0], queries)
    cache_now = jnp.where(moved_here[:, :, :, 0], arrived[1], latent_cache)
    fresh_now = jnp.where(moved_here[:, :, :, 0], arrived[2], fresh_latent)
    lengths_now = jnp.where(moved_flag, arrived[3], lengths)
    latent_out = attend_block(queries_now, cache_now, fresh_now, lengths_now)
    heads_local = value_up_matrix.shape[0]
    model_width = output_weight.shape[1]
    head_weight = output_weight.reshape(heads_local, value_up_matrix.shape[2], model_width)
    value_rows = jnp.einsum(
        "olfb,fbw->olfw",
        lax.all_to_all(latent_out, "ffn", split_axis=2, concat_axis=0, tiled=True),
        value_up_matrix,
        preferred_element_type=jnp.float32,
    ).astype(jnp.bfloat16)
    partial_out = jnp.einsum(
        "rshv,hvd->rsd", value_rows, head_weight, preferred_element_type=jnp.float32
    )
    req_dev = residual.shape[0]
    steps_here = residual.shape[1]
    ffn_index = lax.axis_index("ffn")
    local_token_rows = residual.astype(jnp.float32)
    placed_rows = lax.dynamic_update_slice(
        jnp.zeros_like(partial_out), local_token_rows, (ffn_index * req_dev, 0, 0)
    )
    state_rows = lax.psum(partial_out + placed_rows, "ffn")
    own_state = lax.dynamic_slice_in_dim(state_rows, ffn_index * req_dev, req_dev, 0)
    normed_rows = rms_normalize(state_rows, norm_gain)
    attended = own_state.astype(jnp.bfloat16)
    row_req = normed_rows.shape[0]
    row_tokens = row_req * steps_here
    normed_flat = normed_rows.reshape(row_tokens, model_width)
    expert_count = router.shape[1]
    logits = jnp.dot(normed_flat, router, preferred_element_type=jnp.float32)
    affinity = jax.nn.sigmoid(logits)
    ids_flat = expert_ids.reshape(row_tokens, expert_ids.shape[2])
    onehot = ids_flat[:, :, None] == lax.broadcasted_iota(jnp.int32, (1, 1, expert_count), 2)
    chosen = jnp.sum(jnp.where(onehot, affinity[:, None, :], 0.0), axis=2)
    gate_fraction_value = 2.5 * chosen / jnp.sum(chosen, axis=1, keepdims=True)
    routed_here = ids_flat == ffn_index
    token_weight = jnp.sum(jnp.where(routed_here, gate_fraction_value, 0.0), axis=1)
    token_hit = jnp.sum(routed_here.astype(jnp.int32), axis=1)
    slot_rank = jnp.cumsum(token_hit) - 1
    capacity = 4 * steps_here * req_dev
    slot_ids = lax.broadcasted_iota(jnp.int32, (capacity, row_tokens), 0)
    selector = ((token_hit[None, :] == 1) & (slot_rank[None, :] == slot_ids)).astype(jnp.bfloat16)
    expert_input = jnp.dot(selector, normed_flat, preferred_element_type=jnp.float32).astype(
        jnp.bfloat16
    )
    gate_local = gate_weight[0]
    up_local = up_weight[0]
    down_local = down_weight[0]
    rows_in = lax.all_gather(expert_input, "attn", axis=0, tiled=True)
    gate_part = jnp.dot(rows_in, gate_local, preferred_element_type=jnp.float32)
    up_part = jnp.dot(rows_in, up_local, preferred_element_type=jnp.float32)
    hidden_all = (jax.nn.silu(gate_part) * up_part).astype(jnp.bfloat16)
    rows_in = hidden_all
    expert_rows = lax.psum_scatter(
        jnp.dot(rows_in, down_local, preferred_element_type=jnp.float32),
        "attn",
        scatter_dimension=0,
        tiled=True,
    ).astype(jnp.bfloat16)
    returned = (
        jnp.einsum("ct,cd->td", selector, expert_rows, preferred_element_type=jnp.float32)
        * token_weight[:, None]
    )
    summed = lax.psum_scatter(
        returned.reshape(row_req, steps_here, model_width), "ffn", scatter_dimension=0, tiled=True
    )
    return (attended, summed.astype(jnp.bfloat16))


def solution(mesh):
    return jax.shard_map(
        local,
        mesh=mesh,
        in_specs=(
            P(("attn", "ffn"), None, None, None),
            P(("attn", "ffn"), None, None),
            P(("attn", "ffn"), None, None),
            P(("attn", "ffn")),
            P("ffn", None),
            P(("attn", "ffn"), None, None),
            P("ffn", None, None),
            P("ffn", None),
            P(),
            P(),
            P("attn", None, None),
            P("ffn", None, "attn"),
            P("ffn", None, "attn"),
            P("ffn", "attn", None),
        ),
        out_specs=(P(("attn", "ffn"), None, None), P(("attn", "ffn"), None, None)),
        check_vma=False,
    )
```

profile of v0, /device:TPU:0, one launch (start us, length us, event | category | flops | bytes accessed | tf_op | source)
XLA Modules:
  0.0 625.4 jit_solution(17319362532799770855)
XLA Ops:
  7.2 1.7 collective-permute-start.3
  10.5 7.7 %copy.103 = bf16[8,512,576]{2,1,0:T(8,128)(2,1)} copy(bf16[8,512,576]{1,2,0:T(8,128)(2,1)} %param.15) | data formatting | bytes 9437184 | tf_op args[1]
  18.3 58.3 %collective-permute-done = s32[8]{0:T(128)S(1)} collective-permute-done((s32[8]{0:T(128)}, s32[8]{0:T(128)S(1)}, u32[]{:S(2)}, u32[]{:S(2)}) %collective-permute-start) | collective-permute-done | bytes 64 | tf_op jit(solution)/shard_map/ppermute | solution.py:15
  78.8 7.7 %copy.102 = bf16[8,512,576]{2,1,0:T(8,128)(2,1)} copy(bf16[8,512,576]{1,2,0:T(8,128)(2,1)} %collective-permute-done.2) | data formatting | bytes 9437184 | tf_op jit(solution)/shard_map/ppermute | solution.py:15
  86.6 4.7 broadcast_select_fusion
  91.2 1.9 fusion.8
  97.2 8.1 %all-to-all-start = ((bf16[8,2,64,512]{3,0,1,2:T(8,128)(2,1)}), bf16[8,2,64,512]{3,0,1,2:T(8,128)(2,1)S(1)}, u32[]{:S(2)}, u32[]{:S(2)}) async-start(bf16[8,2,64,512]{3,0,1,2:T(8,128)(2,1)} %copy.107), calls=%async_computation | async-start | bytes 2097152 | tf_op jit(solution)/shard_map/all_to_all | solution.py:85
  105.4 15.1 %all-to-all-done = bf16[8,2,64,512]{3,0,1,2:T(8,128)(2,1)S(1)} async-done(((bf16[8,2,64,512]{3,0,1,2:T(8,128)(2,1)}), bf16[8,2,64,512]{3,0,1,2:T(8,128)(2,1)S(1)}, u32[]{:S(2)}, u32[]{:S(2)}) %all-to-all-start) | async-done | bytes 1048608 | tf_op jit(solution)/shard_map/all_to_all | solution.py:85
  120.5 6.7 %convolution_bitcast_fusion = f32[128,2,7168]{2,0,1:T(8,128)} fusion(bf16[4,128,7168,1]{2,1,0,3:T(8,128)(2,1)} %bitcast.61, bf16[16,8,2,4,512]{4,1,2,3,0:T(8,128)(2,1)S(1)} %bitcast.62, bf16[4,512,128]{2,1,0:T(8,128)(2,1)S(1)} %copy-done), kind=kOutput, calls=%fused_computation.1 | convolution fusion | flops 2013396992 | bytes 16252928 | tf_op jit(solution)/shard_map/rshv,hvd->rsd/dot_general | solution.py:89
  127.2 1.9 add_dynamic-update-slice_fusion
  130.9 127.7 %all-reduce.4.cloned.1.call-done = f32[128,2,7168]{2,0,1:T(8,128)} async-done(((f32[128,2,7168]{2,0,1:T(8,128)}), f32[128,2,7168]{2,0,1:T(8,128)}) %all-reduce.4.cloned.1.call-update) | async-done | bytes 7340048 | tf_op jit(solution)/shard_map/psum | solution.py:99
  258.7 3.8 multiply_reduce_fusion
  264.8 5.6 copy.113
  270.4 8.4 %reshape.169 = bf16[256,7168]{1,0:T(8,128)(2,1)} reshape(bf16[128,2,7168]{2,1,0:T(2,128)(2,1)} %copy.113) | data formatting | bytes 7340032 | tf_op jit(solution)/shard_map/reshape | solution.py:105
  278.8 3.7 convolution_convert_fusion
  282.8 44.9 %all-gather.2.cloned.1.call-done = bf16[512,7168]{1,0:T(8,128)(2,1)} async-done(((bf16[64,7168]{1,0:T(8,128)(2,1)}), bf16[512,7168]{1,0:T(8,128)(2,1)}) %all-gather.2.cloned.1.call-update) | async-done | bytes 7340048 | tf_op jit(solution)/shard_map/all_gather | solution.py:126
  327.7 6.2 fusion.6
  333.9 18.2 %fusion.2 = f32[512,7168]{1,0:T(8,128)} fusion(bf16[1,256,7168]{2,1,0:T(8,128)(2,1)} %param.27, bf16[512,7168]{1,0:T(8,128)(2,1)} %all-gather.2.cloned.1.call-done, bf16[1,7168,256]{2,1,0:T(8,128)(2,1)} %param.26, f32[512,256]{1,0:T(8,128)S(1)} %fusion.6), kind=kOutput, calls=%fused_computation.8 | convolution fusion | flops 3758882816 | bytes 29884416 | tf_op jit(solution)/shard_map/dot_general | solution.py:132
  356.0 3.1 fusion.21
  359.9 74.9 %reduce-scatter.2.cloned.1.call-done = f32[64,7168]{1,0:T(8,128)} async-done(((f32[512,7168]{1,0:T(8,128)}), f32[64,7168]{1,0:T(8,128)}) %reduce-scatter.2.cloned.1.call-update) | async-done | bytes 1835024 | tf_op jit(solution)/shard_map/reduce_scatter | solution.py:131
  434.8 5.6 convolution_multiply_fusion
  440.4 9.3 %reshape.170 = f32[128,2,7168]{2,1,0:T(2,128)} reshape(f32[256,7168]{1,0:T(8,128)} %convolution_multiply_fusion) | data formatting | bytes 14680064 | tf_op jit(solution)/shard_map/reshape | solution.py:142
  449.8 167.4 %all-reduce.5 = bf16[128,2,7168]{2,1,0:T(2,128)(2,1)} all-reduce(f32[128,2,7168]{2,1,0:T(2,128)} %reshape.170), channel_id=3, replica_groups=mesh['attn'=8,'ffn'=16] {'ffn'}, use_global_device_ids=true, to_apply=%region_13.14.clone | all-reduce | flops 1835008 | bytes 11010048
  617.1 1.8 dynamic-slice_convert_fusion
  (79 shorter events, 16.3 us)
Async XLA Ops:
  7.2 113.4 %copy-start = (bf16[4,512,128]{2,1,0:T(8,128)(2,1)S(1)}, bf16[4,512,128]{2,1,0:T(8,128)(2,1)}, u32[]{:S(2)}) copy-start(bf16[4,512,128]{2,1,0:T(8,128)(2,1)} %param.20) | copy-start | bytes 1572868
  7.2 69.5 %copy-start.7 = (bf16[8,2,576]{2,1,0:T(2,128)(2,1)S(1)}, bf16[8,2,576]{2,1,0:T(2,128)(2,1)}, u32[]{:S(2)}) copy-start(bf16[8,2,576]{2,1,0:T(2,128)(2,1)} %param.16) | copy-start | bytes 55300
  7.2 69.6 %copy-start.3 = (bf16[8,2,64,576]{3,2,1,0:T(8,128)(2,1)S(1)}, bf16[8,2,64,576]{3,2,1,0:T(8,128)(2,1)}, u32[]{:S(2)}) copy-start(bf16[8,2,64,576]{3,2,1,0:T(8,128)(2,1)} %param.14) | copy-start | bytes 3538948
  7.2 69.4 %copy-start.10 = (s32[8]{0:T(128)S(1)}, s32[8]{0:T(128)}, u32[]{:S(2)}) copy-start(s32[8]{0:T(128)} %param.17) | copy-start | bytes 100
  7.2 11.0 %copy-start.9 = (s32[1,8]{1,0:T(1,128)S(1)}, s32[1,8]{1,0:T(1,128)}, u32[]{:S(2)}) copy-start(s32[1,8]{1,0:T(1,128)} %param.18) | copy-start | bytes 100
  7.2 71.6 %collective-permute-start.2 = (bf16[8,512,576]{1,2,0:T(8,128)(2,1)}, bf16[8,512,576]{1,2,0:T(8,128)(2,1)}, u32[]{:S(2)}, u32[]{:S(2)}) collective-permute-start(bf16[8,512,576]{1,2,0:T(8,128)(2,1)} %param.15), channel_id=1, source_target_pairs={{0,16},{16,32},{32,48},{48,64},{64,80},{80,96},{96,112},{112,0},{1... | collective-permute-start | bytes 14155784 | tf_op jit(solution)/shard_map/ppermute | solution.py:15
  7.2 69.4 %collective-permute-start.3 = (bf16[8,2,576]{2,1,0:T(2,128)(2,1)}, bf16[8,2,576]{2,1,0:T(2,128)(2,1)S(1)}, u32[]{:S(2)}, u32[]{:S(2)}) collective-permute-start(bf16[8,2,576]{2,1,0:T(2,128)(2,1)} %param.16), channel_id=1, source_target_pairs={{0,16},{16,32},{32,48},{48,64},{64,80},{80,96},{96,112},{112,0},{1... | collective-permute-start | bytes 55304 | tf_op jit(solution)/shard_map/ppermute | solution.py:15
  8.9 67.8 %collective-permute-start.1 = (bf16[8,2,64,576]{3,2,1,0:T(8,128)(2,1)}, bf16[8,2,64,576]{3,2,1,0:T(8,128)(2,1)}, u32[]{:S(2)}, u32[]{:S(2)}) collective-permute-start(bf16[8,2,64,576]{3,2,1,0:T(8,128)(2,1)} %param.14), channel_id=1, source_target_pairs={{0,16},{16,32},{32,48},{48,64},{64,80},{80,96},{96,112},{112,0},{1... | collective-permute-start | bytes 3538952 | tf_op jit(solution)/shard_map/ppermute | solution.py:15
  9.0 67.6 %collective-permute-start = (s32[8]{0:T(128)}, s32[8]{0:T(128)S(1)}, u32[]{:S(2)}, u32[]{:S(2)}) collective-permute-start(s32[8]{0:T(128)} %param.17), channel_id=1, source_target_pairs={{0,16},{16,32},{32,48},{48,64},{64,80},{80,96},{96,112},{112,0},{1... | collective-permute-start | bytes 104 | tf_op jit(solution)/shard_map/ppermute | solution.py:15
  97.2 23.3 %all-to-all-start = ((bf16[8,2,64,512]{3,0,1,2:T(8,128)(2,1)}), bf16[8,2,64,512]{3,0,1,2:T(8,128)(2,1)S(1)}, u32[]{:S(2)}, u32[]{:S(2)}) async-start(bf16[8,2,64,512]{3,0,1,2:T(8,128)(2,1)} %copy.107), calls=%async_computation | async-start | bytes 2097152 | tf_op jit(solution)/shard_map/all_to_all | solution.py:85
  105.3 153.3 %all-reduce.4.cloned.1.call-start = ((), (), s32[]{:S(2)}) async-start(), calls=%async_computation.2 | async-start | bytes 14680064 | tf_op jit(solution)/shard_map/psum | solution.py:99
  120.5 6.7 %copy-start.4 = (bf16[8,2,7168]{2,1,0:T(2,128)(2,1)S(1)}, bf16[8,2,7168]{2,1,0:T(2,128)(2,1)}, u32[]{:S(2)}) copy-start(bf16[8,2,7168]{2,1,0:T(2,128)(2,1)} %param.19) | copy-start | bytes 688132
  129.1 0.7 copy-start.8
  129.1 133.4 %copy-start.6 = (f32[7168]{0:T(1024)S(1)}, f32[7168]{0:T(1024)}, u32[]{:S(2)}) copy-start(f32[7168]{0:T(1024)} %param.22) | copy-start | bytes 86020
  129.1 198.6 %all-gather.2.cloned.1.call-start = ((), (), s32[]{:S(2)}) async-start(), calls=%async_computation.3 | async-start | bytes 8257536 | tf_op jit(solution)/shard_map/all_gather | solution.py:126
  258.7 5.2 copy-start.2
  282.6 152.2 %reduce-scatter.2.cloned.1.call-start = ((), (), s32[]{:S(2)}) async-start(), calls=%async_computation.4 | async-start | bytes 16515072 | tf_op jit(solution)/shard_map/reduce_scatter | solution.py:131
  352.1 0.7 copy-start.11
  352.1 3.9 copy-start.5
  440.4 178.5 %copy-start.1 = (bf16[4,512,128]{2,1,0:T(8,128)(2,1)S(1)}, bf16[4,512,128]{2,1,0:T(8,128)(2,1)}, u32[]{:S(2)}) copy-start(bf16[4,512,128]{2,1,0:T(8,128)(2,1)} %param.20) | copy-start | bytes 1572868
Sparse Core Ops, SparseCore 0:
  129.2 129.4 all-reduce.3
  282.7 44.9 all-gather.1
  352.3 82.5 reduce-scatter.1
where the time goes:
time: 627 us; the launch traced here: 625 us
  waiting for transfers between devices  321 us (51%)
  blocking collectives  167 us (27%)
  local copies, waits for them, and re-layouts  48.5 us (8%)
  matrix products  47.7 us (8%)
  between operations  14.7 us (2%)
  other arithmetic  14.2 us (2%)
  starting transfers between devices  12 us (2%)
    unnamed x1, blocking collectives  167 us
    psum x1, waiting for transfers between devices, local(): state_rows = lax.psum(partial_out + placed_rows, 'ffn')  128 us
    reduce_scatter x1, waiting for transfers between devices, local(): lax.psum_scatter(jnp.dot(rows_in, down_local, preferred_element_type=jnp....  74.9 us
    ppermute x4, waiting for transfers between devices, shifted(): lax.ppermute(value, axis, [(i, (i + by) % count) for i in range(count)])  58.3 us
    all_gather x1, waiting for transfers between devices, local(): rows_in = lax.all_gather(expert_input, 'attn', axis=0, tiled=True)  44.9 us
    dot_general x1, matrix products, local(): jnp.dot(rows_in, down_local, preferred_element_type=jnp.float32)  18.2 us
    all_to_all x1, waiting for transfers between devices, local(): lax.all_to_all(latent_out, 'ffn', split_axis=2, concat_axis=0, tiled=True)  15.1 us
  transfers between devices with their start and end apart: 8, of which 5 were waited for; matrix products, arithmetic and copies ran while one was open for 3% of the time, Pallas kernels for 0%

commit v1 on v0

--- a/solution.py
+++ b/solution.py
@@ -69,14 +69,9 @@
     up_weight,
     down_weight,
 ):
-    moved_flag = handoff[0] == 1
-    moved_here = moved_flag[:, None, None, None]
-    arrived = shifted((queries, latent_cache, fresh_latent, lengths), "attn", 1)
-    queries_now = jnp.where(moved_here, arrived[0], queries)
-    cache_now = jnp.where(moved_here[:, :, :, 0], arrived[1], latent_cache)
-    fresh_now = jnp.where(moved_here[:, :, :, 0], arrived[2], fresh_latent)
-    lengths_now = jnp.where(moved_flag, arrived[3], lengths)
-    latent_out = attend_block(queries_now, cache_now, fresh_now, lengths_now)
+    moved_here = (handoff[0] == 1)[:, None, None, None]
+    latent_home = attend_block(queries, latent_cache, fresh_latent, lengths)
+    latent_out = jnp.where(moved_here, shifted(latent_home, "attn", 1), latent_home)
     heads_local = value_up_matrix.shape[0]
     model_width = output_weight.shape[1]
     head_weight = output_weight.reshape(heads_local, value_up_matrix.shape[2], model_width)
@@ -92,15 +87,18 @@
     req_dev = residual.shape[0]
     steps_here = residual.shape[1]
     ffn_index = lax.axis_index("ffn")
-    local_token_rows = residual.astype(jnp.float32)
-    placed_rows = lax.dynamic_update_slice(
-        jnp.zeros_like(partial_out), local_token_rows, (ffn_index * req_dev, 0, 0)
+    own_state = lax.psum_scatter(
+        partial_out.astype(jnp.bfloat16).reshape(-1, model_width),
+        "ffn",
+        scatter_dimension=0,
+        tiled=True,
+    ).astype(jnp.float32).reshape(residual.shape) + residual.astype(jnp.float32)
+    attended = own_state.astype(jnp.bfloat16)
+    normed_own = rms_normalize(own_state, norm_gain)
+    row_req = partial_out.shape[0]
+    normed_rows = lax.all_gather(
+        normed_own.reshape(req_dev * steps_here, model_width), "ffn", axis=0, tiled=True
     )
-    state_rows = lax.psum(partial_out + placed_rows, "ffn")
-    own_state = lax.dynamic_slice_in_dim(state_rows, ffn_index * req_dev, req_dev, 0)
-    normed_rows = rms_normalize(state_rows, norm_gain)
-    attended = own_state.astype(jnp.bfloat16)
-    row_req = normed_rows.shape[0]
     row_tokens = row_req * steps_here
     normed_flat = normed_rows.reshape(row_tokens, model_width)
     expert_count = router.shape[1]
@@ -129,19 +127,19 @@
     hidden_all = (jax.nn.silu(gate_part) * up_part).astype(jnp.bfloat16)
     rows_in = hidden_all
     expert_rows = lax.psum_scatter(
-        jnp.dot(rows_in, down_local, preferred_element_type=jnp.float32),
+        jnp.dot(rows_in, down_local, preferred_element_type=jnp.float32).astype(jnp.bfloat16),
         "attn",
         scatter_dimension=0,
         tiled=True,
-    ).astype(jnp.bfloat16)
+    )
     returned = (
         jnp.einsum("ct,cd->td", selector, expert_rows, preferred_element_type=jnp.float32)
         * token_weight[:, None]
     )
     summed = lax.psum_scatter(
-        returned.reshape(row_req, steps_here, model_width), "ffn", scatter_dimension=0, tiled=True
+        returned.astype(jnp.bfloat16), "ffn", scatter_dimension=0, tiled=True
     )
-    return (attended, summed.astype(jnp.bfloat16))
+    return (attended, summed.reshape(residual.shape))
 
 
 def solution(mesh):

time: 627 us -> 413 us (0.66)
  blocking collectives: 167 us -> 23.1 us
  local copies, waits for them, and re-layouts: 48.5 us -> 22.8 us
  waiting for transfers between devices: 321 us -> 301 us
  starting transfers between devices: 12 us -> 0.62 us
  other arithmetic: 14.2 us -> 4.18 us
    unnamed x1 -> x0, blocking collectives: 167 us -> none
    reduce_scatter x0 -> x2, waiting for transfers between devices: none -> 150 us  [the longest x1 76.4 us: local(): lax.psum_scatter(returned.astype(jnp.bfloat16), 'ffn', scatter_dimension=...]
    psum x1 -> x0, waiting for transfers between devices: 128 us -> none  [local(): state_rows = lax.psum(partial_out + placed_rows, 'ffn')]
    all_gather x0 -> x1, waiting for transfers between devices: none -> 47.9 us  [local(): lax.all_gather(normed_own.reshape(req_dev * steps_here, model_width), 'ff...]
    ppermute x4 -> x1, waiting for transfers between devices: 58.3 us -> 15.4 us  [shifted(): lax.ppermute(value, axis, [(i, (i + by) % count) for i in range(count)])]
    reduce_scatter x1, waiting for transfers between devices: 74.9 us -> 42.9 us  [local(): lax.psum_scatter(jnp.dot(rows_in, down_local, preferred_element_type=jnp....]
    all_to_all x0 -> x1, blocking collectives: none -> 23.1 us  [local(): lax.all_to_all(latent_out, 'ffn', split_axis=2, concat_axis=0, tiled=True)]
    all_to_all x1 -> x0, waiting for transfers between devices: 15.1 us -> none  [local(): lax.all_to_all(latent_out, 'ffn', split_axis=2, concat_axis=0, tiled=True)]
  transfers between devices with their start and end apart: 8 -> 6, of which waited for: 5 -> 6; matrix products, arithmetic and copies ran while one was open for 3% -> 1% of each run, Pallas kernels for 0% -> 0%
where the time goes in v1:
time: 413 us
  waiting for transfers between devices  301 us (73%)
  matrix products  46.6 us (11%)
  blocking collectives  23.1 us (6%)
  local copies, waits for them, and re-layouts  22.8 us (6%)
  between operations  14 us (3%)
  other arithmetic  4.18 us (1%)
    reduce_scatter x1, waiting for transfers between devices, local(): lax.psum_scatter(returned.astype(jnp.bfloat16), 'ffn', scatter_dimension=...  76.4 us
    reduce_scatter x1, waiting for transfers between devices, local(): lax.psum_scatter(partial_out.astype(jnp.bfloat16).reshape(-1, model_width...  74 us
    all_gather x1, waiting for transfers between devices, local(): lax.all_gather(normed_own.reshape(req_dev * steps_here, model_width), 'ff...  47.9 us
    all_gather x1, waiting for transfers between devices, local(): rows_in = lax.all_gather(expert_input, 'attn', axis=0, tiled=True)  44.4 us
    reduce_scatter x1, waiting for transfers between devices, local(): lax.psum_scatter(jnp.dot(rows_in, down_local, preferred_element_type=jnp....  42.9 us
    all_to_all x1, blocking collectives, local(): lax.all_to_all(latent_out, 'ffn', split_axis=2, concat_axis=0, tiled=True)  23.1 us
    dot_general x1, matrix products, local(): jnp.dot(rows_in, down_local, preferred_element_type=jnp.float32)  16 us
    ppermute x1, waiting for transfers between devices, shifted(): lax.ppermute(value, axis, [(i, (i + by) % count) for i in range(count)])  15.4 us
  transfers between devices with their start and end apart: 6, of which 6 were waited for; matrix products, arithmetic and copies ran while one was open for 1% of the time, Pallas kernels for 0%

profile of v1, /device:TPU:0, one launch (start us, length us, event | category | flops | bytes accessed | tf_op | source)
XLA Modules:
  0.0 412.5 jit_solution(5280940348279250540)
XLA Ops:
  7.3 0.8 iota_compare_fusion.2
  8.5 1.4 fusion.52
  9.9 3.5 fusion.9
  14.2 2.1 fusion.2
  17.4 15.4 %collective-permute-done = bf16[8,2,64,512]{3,0,1,2:T(8,128)(2,1)S(1)} collective-permute-done((bf16[8,2,64,512]{3,0,1,2:T(8,128)(2,1)S(1)}, bf16[8,2,64,512]{3,0,1,2:T(8,128)(2,1)S(1)}, u32[]{:S(2)}, u32[]{:S(2)}) %collective-permute-start) | collective-permute-done | bytes 1048608 | tf_op jit(solution)/shard_map/ppermute | solution.py:15
  32.8 0.7 broadcast_select_fusion
  33.5 23.1 %all_to_all.18 = bf16[8,2,64,512]{3,0,1,2:T(8,128)(2,1)S(1)} all-to-all(bf16[8,2,64,512]{3,0,1,2:T(8,128)(2,1)S(1)} %broadcast_select_fusion), channel_id=1, replica_groups=mesh['attn'=8,'ffn'=16] {'ffn'}, dimensions={2} | all-to-all | bytes 2097152 | tf_op jit(solution)/shard_map/all_to_all | solution.py:80
  56.6 6.1 %fusion = bf16[128,2,7168]{2,0,1:T(8,128)(2,1)} fusion(bf16[4,128,7168,1]{2,1,0,3:T(8,128)(2,1)} %bitcast.63, bf16[16,8,2,4,512]{4,1,2,3,0:T(8,128)(2,1)S(1)} %bitcast.66, bf16[4,512,128]{2,1,0:T(8,128)(2,1)S(1)} %copy-done.2), kind=kOutput, calls=%fused_computation.3 | convolution fusion | flops 2015232000 | bytes 12582912 | tf_op jit(solution)/shard_map/rshv,hvd->rsd/dot_general | solution.py:84
  62.7 7.6 %copy.89 = bf16[128,2,7168]{2,1,0:T(2,128)(2,1)} copy(bf16[128,2,7168]{2,0,1:T(8,128)(2,1)} %fusion) | data formatting | bytes 7340032 | tf_op jit(solution)/shard_map/convert_element_type | solution.py:91
  70.3 8.4 %reshape.171 = bf16[256,7168]{1,0:T(8,128)(2,1)} reshape(bf16[128,2,7168]{2,1,0:T(2,128)(2,1)} %copy.89) | data formatting | bytes 7340032 | tf_op jit(solution)/shard_map/reshape | solution.py:91
  78.9 74.0 %reduce-scatter.4.cloned.1.call-done = bf16[16,7168]{1,0:T(8,128)(2,1)} async-done(((bf16[256,7168]{1,0:T(8,128)(2,1)}), bf16[16,7168]{1,0:T(8,128)(2,1)}) %reduce-scatter.4.cloned.1.call-update) | async-done | bytes 229392 | tf_op jit(solution)/shard_map/reduce_scatter | solution.py:90
  152.9 1.2 reshape.179
  154.6 1.1 multiply_convert_fusion
  155.7 0.8 reshape.176
  157.7 47.9 %all-gather.3.cloned.1.call-done = bf16[256,7168]{1,0:T(8,128)(2,1)} async-done(((bf16[16,7168]{1,0:T(8,128)(2,1)}), bf16[256,7168]{1,0:T(8,128)(2,1)}) %all-gather.3.cloned.1.call-update) | async-done | bytes 3670032 | tf_op jit(solution)/shard_map/all_gather | solution.py:99
  205.6 3.7 convolution_convert_fusion.1
  209.4 44.4 %all-gather.5.cloned.1.call-done = bf16[512,7168]{1,0:T(8,128)(2,1)} async-done(((bf16[64,7168]{1,0:T(8,128)(2,1)}), bf16[512,7168]{1,0:T(8,128)(2,1)}) %all-gather.5.cloned.1.call-update) | async-done | bytes 7340048 | tf_op jit(solution)/shard_map/all_gather | solution.py:124
  253.8 6.2 %fusion.7 = f32[512,256]{1,0:T(8,128)S(1)} fusion(bf16[512,7168]{1,0:T(8,128)(2,1)} %all-gather.5.cloned.1.call-done, bf16[1,7168,256]{2,1,0:T(8,128)(2,1)} %param.25), kind=kOutput, calls=%fused_computation.11 | convolution fusion | flops 1879048192 | bytes 11534336 | tf_op jit(solution)/shard_map/dot_general | solution.py:125
  260.0 16.0 %convolution_convert_fusion = bf16[512,7168]{1,0:T(8,128)(2,1)} fusion(bf16[1,256,7168]{2,1,0:T(8,128)(2,1)} %param.27, bf16[512,7168]{1,0:T(8,128)(2,1)} %all-gather.5.cloned.1.call-done, bf16[1,7168,256]{2,1,0:T(8,128)(2,1)} %param.26, f32[512,256]{1,0:T(8,128)S(1)} %fusion.7), kind=kOutput, calls=%fused_computation | convolution fusion | flops 3762552832 | bytes 22544384 | tf_op jit(solution)/shard_map/dot_general | solution.py:130
  276.9 3.1 fusion.20
  280.8 42.9 %reduce-scatter.6.cloned.1.call-done = bf16[64,7168]{1,0:T(8,128)(2,1)} async-done(((bf16[512,7168]{1,0:T(8,128)(2,1)}), bf16[64,7168]{1,0:T(8,128)(2,1)}) %reduce-scatter.6.cloned.1.call-update) | async-done | bytes 917520 | tf_op jit(solution)/shard_map/reduce_scatter | solution.py:129
  323.7 4.1 %fusion.1 = bf16[256,7168]{1,0:T(8,128)(2,1)} fusion(bf16[64,7168]{1,0:T(8,128)(2,1)} %reduce-scatter.6.cloned.1.call-done, f32[256]{0:T(256)S(1)} %mul.72, s32[256]{0:T(256)S(1)} %add_bitcast_fusion, pred[256]{0:T(512)(128)(4,1)S(1)} %eq.61), kind=kOutput, calls=%fused_computation.4 | convolution fusion | flops 238583808 | bytes 4589824 | tf_op jit(solution)/shard_map/ct,cd->td/dot_general | solution.py:136
  327.9 76.4 %reduce-scatter.8.cloned.1.call-done = bf16[16,7168]{1,0:T(8,128)(2,1)} async-done(((bf16[256,7168]{1,0:T(8,128)(2,1)}), bf16[16,7168]{1,0:T(8,128)(2,1)}) %reduce-scatter.8.cloned.1.call-update) | async-done | bytes 229392 | tf_op jit(solution)/shard_map/reduce_scatter | solution.py:139
  404.3 1.7 reshape.177
  (68 shorter events, 5.9 us)
Async XLA Ops:
  7.2 1.3 copy-start
  7.2 145.7 %reduce-scatter.4.cloned.1.call-start = ((), (), s32[]{:S(2)}) async-start(), calls=%async_computation.4 | async-start | bytes 3899392 | tf_op jit(solution)/shard_map/reduce_scatter | solution.py:90
  8.5 5.6 %slice-start = ((s8[4718592]{0:T(1024)(128)(4,1)}), s8[4194304]{0:T(1024)(128)(4,1)S(1)}, s32[]{:S(2)}) async-start(s8[4718592]{0:T(1024)(128)(4,1)} %bitcast.64), calls=%async_computation.9 | async-start | bytes 8388608
  9.9 4.2 %slice-start.1 = ((s8[4718592]{0:T(1024)(128)(4,1)}), s8[524288]{0:T(1024)(128)(4,1)S(1)}, s32[]{:S(2)}) async-start(s8[4718592]{0:T(1024)(128)(4,1)} %bitcast.64), calls=%async_computation.10 | async-start | bytes 1048576
  14.2 2.1 copy-start.5
  16.3 1.1 copy-start.8
  16.8 39.8 %copy-start.2 = (bf16[4,512,128]{2,1,0:T(8,128)(2,1)S(1)}, bf16[4,512,128]{2,1,0:T(8,128)(2,1)}, u32[]{:S(2)}) copy-start(bf16[4,512,128]{2,1,0:T(8,128)(2,1)} %param.20) | copy-start | bytes 1572868
  17.4 15.4 %collective-permute-start = (bf16[8,2,64,512]{3,0,1,2:T(8,128)(2,1)S(1)}, bf16[8,2,64,512]{3,0,1,2:T(8,128)(2,1)S(1)}, u32[]{:S(2)}, u32[]{:S(2)}) collective-permute-start(bf16[8,2,64,512]{3,0,1,2:T(8,128)(2,1)S(1)} %copy.85), channel_id=1, source_target_pairs={{0,16},{16,32},{32,48},{48,64},{64,80},{80,96},{96,112},{112,0},{1... | collective-permute-start | bytes 3145736 | tf_op jit(solution)/shard_map/ppermute | solution.py:15
  78.7 75.5 %copy-start.3 = (bf16[8,2,7168]{2,1,0:T(2,128)(2,1)S(1)}, bf16[8,2,7168]{2,1,0:T(2,128)(2,1)}, u32[]{:S(2)}) copy-start(bf16[8,2,7168]{2,1,0:T(2,128)(2,1)} %param.19) | copy-start | bytes 688132
  78.7 75.9 %copy-start.6 = (f32[7168]{0:T(1024)S(1)}, f32[7168]{0:T(1024)}, u32[]{:S(2)}) copy-start(f32[7168]{0:T(1024)} %param.22) | copy-start | bytes 86020
  78.7 77.8 %copy-start.7 = (s32[128,2,2]{0,2,1:T(2,128)S(1)}, s32[128,2,2]{0,2,1:T(2,128)}, u32[]{:S(2)}) copy-start(s32[128,2,2]{0,2,1:T(2,128)} %param.24) | copy-start | bytes 6148
  78.7 126.9 %all-gather.3.cloned.1.call-start = ((), (), s32[]{:S(2)}) async-start(), calls=%async_computation.5 | async-start | bytes 3899392 | tf_op jit(solution)/shard_map/all_gather | solution.py:99
  156.5 97.4 %all-gather.5.cloned.1.call-start = ((), (), s32[]{:S(2)}) async-start(), calls=%async_computation.6 | async-start | bytes 8257536 | tf_op jit(solution)/shard_map/all_gather | solution.py:124
  209.4 114.3 %reduce-scatter.6.cloned.1.call-start = ((), (), s32[]{:S(2)}) async-start(), calls=%async_computation.7 | async-start | bytes 8257536 | tf_op jit(solution)/shard_map/reduce_scatter | solution.py:129
  276.0 0.9 copy-start.4
  276.0 128.3 %reduce-scatter.8.cloned.1.call-start = ((), (), s32[]{:S(2)}) async-start(), calls=%async_computation.8 | async-start | bytes 3899392 | tf_op jit(solution)/shard_map/reduce_scatter | solution.py:139
  280.7 125.4 %copy-start.1 = (bf16[8,2,64,576]{3,2,1,0:T(8,128)(2,1)S(1)}, bf16[8,2,64,576]{3,2,1,0:T(8,128)(2,1)}, u32[]{:S(2)}) copy-start(bf16[8,2,64,576]{3,2,1,0:T(8,128)(2,1)} %param.14) | copy-start | bytes 3538948
Sparse Core Ops, SparseCore 0:
  78.8 74.0 reduce-scatter.3
  156.6 48.9 all-gather.2
  209.5 44.2 all-gather.4
  276.1 47.5 reduce-scatter.5
  328.0 76.2 reduce-scatter.7
